TPU v7x, 128 devices: a whole 4x4x4 slice. The times are simulated.
128 devices in a mesh: gx: 16 (over z, y_lo, core), gy: 8 (over x, y_hi).
Axes of the slice: x: 4, y: 4 (y_hi: 2, y_lo: 2; y = y_hi * 2 + y_lo), z: 4, core: 2. Of those that a mesh axis runs over, the one named last changes fastest.
Arguments:
- source_hat: float32 [2, 3, 256, 256, 256], P(None, None, 'gx', 'gy'), may hold values from -0.0014648438 to 0.0014648438
- particle_start: int32 [3, 262144], P(None, ('gx', 'gy')), may hold values from 0 to 255, as said below
- particle_offset: float32 [3, 262144], P(None, ('gx', 'gy')), may hold values from 0 to 1
- ghost_start: int32 [3, 3, 65536], P(None, None, ('gx', 'gy')), may hold values from 0 to 255, as said below
- ghost_offset: float32 [3, 3, 65536], P(None, None, ('gx', 'gy')), may hold values from 0 to 1, as said below
- ghost_slot: int32 [3, 65536], P(None, ('gx', 'gy')), may hold values from 0 to 2047, as said below
- counts: int32 [128, 4], P(('gx', 'gy')), may hold values from 0 to 2048, as said below
Outputs:
- velocity_far: float32 [3, 262144], P(None, ('gx', 'gy'))
- strain_far: float32 [5, 262144], P(None, ('gx', 'gy'))
Inputs may be any that keep to these rules, and one draw needn't show every extreme that they name: `particle_start`: on device (a, b), a its gx index and b its gy index, every slot's x start lies in [b * 32, (b + 1) * 32) and its z start in [a * 16, (a + 1) * 16). `counts`: row of a device: its live own slots (the slots below this count are live), then the live entries of ghost groups 0, 1, 2 (the entries below each count are live); each ghost count is at most 512. `ghost_slot`: group 0 of device (a, b) lists particles of device (a, b - 1), group 1 of (a - 1, b), group 2 of (a - 1, b - 1), indices modulo the axis sizes; every entry is a slot index of that owner, below 2048; its live entries name distinct live slots of that owner, and they are exactly the owner's live particles whose support reaches the device's brick. `ghost_start`: A live ghost entry repeats the start of the owner's slot that ghost_slot names. `ghost_offset`: A live ghost entry repeats the offset of the owner's slot that ghost_slot names.
All inputs are finite; a program needn't handle non-finite values.
Results may differ from a plain program's by a relative error of at most 0.008.
Values sent between devices are 32-bit elements; how exact they have to be, the bound alone decides.
No kernel may reach another device: no remote copies, remote signals or barrier semaphores. Data moves between devices by JAX's collectives and lax.ppermute only.
A program may use at most 192 MiB of HBM per device.

v0:
```python
import math

import jax
import jax.numpy as jnp
import numpy as np
from jax import lax
from jax.experimental import pallas as pl
from jax.experimental.pallas import tpu as pltpu
from jax.sharding import PartitionSpec as P


F32 = jnp.float32
BF16 = jnp.bfloat16
SUPPORT = 8
GRID = 256
HALF = GRID // 2
N_GX = 16
N_GY = 8
OWN = 2048
GHOST = 512
ROWS = OWN + GHOST
WAVE = 2.0 * math.pi / GRID
WINDOW = 48
BLOCK = 256
CHUNKS = ((0, 2, 1, 3),)
ORDER = (0, 2, 1, 3)
FIELDS = 7
EXTRA = 4
BLOCKS = ROWS // BLOCK
JOBS = N_GY * BLOCKS + 2
HEAD = 3
AHEAD = 8
SLOTS = 8


def numpy_halves(table):
    import ml_dtypes

    high = table.astype(ml_dtypes.bfloat16)
    low = (table - high.astype(np.float64)).astype(ml_dtypes.bfloat16)
    return high, low


def left_triple(table):
    high, low = numpy_halves(table)
    return np.concatenate([high, high, low], axis=-1)


def z_table():
    c1, slab, part, step = np.meshgrid(
        np.arange(2), np.arange(N_GX), np.arange(2), np.arange(4), indexing="ij"
    )
    position = (8 * slab + 2 * step + c1).reshape(-1, 1)
    part = part.reshape(-1, 1)
    angle = (position * np.arange(HALF)[None, :] % HALF) * (2.0 * np.pi / HALF)
    cosine, sine = np.cos(angle), np.sin(angle)
    from_real = np.where(part == 0, cosine, sine)
    from_imag = np.where(part == 0, -sine, cosine)
    return np.concatenate([from_real, from_imag], axis=1)


def x_table(parity):
    modes = 2 * np.arange(HALF) + parity
    angle = (np.arange(HALF)[:, None] * modes[None, :] % GRID) * (2.0 * np.pi / GRID)
    cosine, sine = np.cos(angle), np.sin(angle)
    return np.block([[cosine, -sine], [sine, cosine]])


def y_table():
    index = np.arange(GRID)
    angle = (index[:, None] * index[None, :] % GRID) * (2.0 * np.pi / GRID)
    cosine = np.cos(angle).reshape(N_GY, 1, GRID // N_GY, GRID)
    sine = -np.sin(angle).reshape(N_GY, 1, GRID // N_GY, GRID)
    return np.concatenate([cosine, sine], axis=1).reshape(N_GY, 2 * (GRID // N_GY), GRID)


def y_tables():
    full = y_table()
    high, low = numpy_halves(full)
    none = np.zeros_like(high[..., :SUPPORT])
    near_high, near_low = high[..., :SUPPORT], low[..., :SUPPORT]
    return np.concatenate([high, low, near_high, near_high, near_low, none], axis=-1)


def twiddles():
    angle = np.arange(HALF) * (2.0 * np.pi / GRID)
    table = np.stack([np.cos(angle), np.sin(angle)])
    return np.repeat(table[:, None, :], 32, axis=1).astype(np.float32)


def split(value):
    high = value.astype(BF16)
    return high, (value - high.astype(F32)).astype(BF16)


def signed(index):
    return jnp.where(index < GRID // 2, index, index - GRID).astype(F32)


NT = (((1,), (1,)), ((), ()))
NN = (((1,), (0,)), ((), ()))


def dot(a, b, dims):
    return lax.dot_general(a, b, dims, preferred_element_type=F32)


def z_kernel(groups, source, table, twiddle, *rest):
    outs, even, odd = rest[:-2], rest[-2], rest[-1]
    home = {c: (outs[g], group.index(c)) for g, group in enumerate(groups) for c in group}
    pieces = tuple(home)
    quad = pl.program_id(0)
    with_extra = EXTRA in pieces
    parities = [p for p in range(2) if any(c != EXTRA and c % 2 == p for c in pieces)]
    row = lax.broadcasted_iota(jnp.int32, (32, GRID), 0)
    mode_y = signed(row + lax.axis_index("gy") * 32)
    mode_z = signed(lax.broadcasted_iota(jnp.int32, (32, GRID), 1))
    half_wave_z = 0.5 * WAVE * mode_z
    partial_square = mode_y * mode_y + mode_z * mode_z
    turn_re, turn_im = twiddle[0], twiddle[1]

    def build(k):
        index_x = lax.axis_index("gx") * 16 + quad * 4 + k
        mode_x = jnp.where(index_x < GRID // 2, index_x, index_x - GRID).astype(F32)
        inverse = 1.0 / jnp.maximum(mode_x * mode_x + partial_square, 1.0)
        v = []
        for r in range(2):
            s1, s2, s3 = source[r, 0, k], source[r, 1, k], source[r, 2, k]
            ratio = (s1 * mode_x + s2 * mode_y + s3 * mode_z) * inverse
            v.append((s1 - mode_x * ratio, s2 - mode_y * ratio, s3 - mode_z * ratio))
        rows = [
            (v[0][0], v[1][0], k * 128),
            (v[0][1], v[1][1], k * 128 + 32),
            (v[0][2], v[1][2], k * 128 + 64),
            (-half_wave_z * v[1][0], half_wave_z * v[0][0], k * 128 + 96),
        ]
        if with_extra:
            rows.append((-half_wave_z * v[1][1], half_wave_z * v[0][1], 512 + k * 32))
        for real, imag, start in rows:
            here = slice(start, start + 32)
            for p in parities if start < 512 else range(2):
                if p == 0:
                    re = real[:, :HALF] + real[:, HALF:]
                    im = imag[:, :HALF] + imag[:, HALF:]
                    target = even
                else:
                    re0 = real[:, :HALF] - real[:, HALF:]
                    im0 = imag[:, :HALF] - imag[:, HALF:]
                    re = re0 * turn_re - im0 * turn_im
                    im = re0 * turn_im + im0 * turn_re
                    target = odd
                for r, value in ((0, re), (1, im)):
                    high, low = split(value)
                    target[here, r * HALF : (r + 1) * HALF] = high
                    target[here, GRID + r * HALF : GRID + (r + 1) * HALF] = low
                    target[here, 2 * GRID + r * HALF : 2 * GRID + (r + 1) * HALF] = high

    def transform(pair):
        for p in parities:
            wanted = [c for c in pieces if c != EXTRA and c % 2 == p]
            if not wanted:
                continue
            c_low, c_high = min(wanted) // 2, max(wanted) // 2 + 1
            data = (even, odd)[p][pair * 256 : pair * 256 + 256]
            result = dot(table[c_low * 128 : c_high * 128], data, NT)
            for c in wanted:
                top = (c // 2 - c_low) * 128
                out, at = home[c]
                for side in range(2):
                    out[:, at, side, pair] = result[
                        top : top + 128, side * 128 : side * 128 + 128
                    ].reshape(N_GX, 8, 128)

    build(0)
    build(1)
    transform(0)
    build(2)
    build(3)
    transform(1)
    if with_extra:
        halves = [dot(table[...], data[512:640], NT) for data in (even, odd)]
        v = [halves[c % 2][(c // 2) * 128 : (c // 2) * 128 + 128] for c in range(4)]
        lane = lax.broadcasted_iota(jnp.int32, (128, 128), 1)
        lower64 = lane < 64
        lower32 = (lane & 32) == 0
        p0 = [jnp.where(lower64, v[c], pltpu.roll(v[c + 2], 64, 1)) for c in range(2)]
        p1 = [jnp.where(lower64, pltpu.roll(v[c], 64, 1), v[c + 2]) for c in range(2)]
        out, at = home[EXTRA]
        for k1, p in ((0, p0), (1, p1)):
            q0 = jnp.where(lower32, p[0], pltpu.roll(p[1], 32, 1))
            q1 = jnp.where(lower32, pltpu.roll(p[0], 96, 1), p[1])
            out[:, at, 0, k1] = q0.reshape(N_GX, 8, 128)
            out[:, at, 1, k1] = q1.reshape(N_GX, 8, 128)


def z_stage(groups, source, table, twiddle):
    def kernel(*refs):
        z_kernel(groups, *refs)

    return pl.pallas_call(
        kernel,
        out_shape=tuple(
            jax.ShapeDtypeStruct((N_GX, len(group), 2, 8, 8, 128), F32) for group in groups
        ),
        grid=(4,),
        in_specs=[
            pl.BlockSpec((2, 3, 4, 32, GRID), lambda i: (0, 0, i, 0, 0)),
            pl.BlockSpec((256, 768), lambda i: (0, 0)),
            pl.BlockSpec((2, 32, HALF), lambda i: (0, 0, 0)),
        ],
        out_specs=tuple(
            pl.BlockSpec((N_GX, len(group), 2, 2, 8, 128), lambda i: (0, 0, 0, i, 0, 0))
            for group in groups
        ),
        scratch_shapes=[pltpu.VMEM((640, 768), BF16), pltpu.VMEM((640, 768), BF16)],
        name="z_stage",
    )(source, table, twiddle)


def weight(distance, offset):
    shifted = distance - (SUPPORT // 2 - 1) - offset
    inside = (distance >= 0.0) & (distance < SUPPORT)
    return jnp.where(inside, jnp.exp(-5.6 / SUPPORT * shifted * shifted), 0.0)


def wrapped(distance):
    return jnp.where(distance < 0.0, distance + GRID, distance)


def gather_kernel(counts, start, offset, other_start, other_offset, out, packed):
    own, ghosts = counts[0, 0], counts[0, 2]
    lane = lax.broadcasted_iota(jnp.int32, (8, ROWS), 1)
    packed[...] = jnp.zeros_like(packed)
    packed[0:3, :GHOST] = other_start[:, 1].astype(F32)
    packed[3:6, :GHOST] = other_offset[:, 1]
    moved = pltpu.roll(packed[...], own, 1)
    packed[0:3, :OWN] = start[...].astype(F32)
    packed[3:6, :OWN] = offset[...]
    out[...] = jnp.where(lane < own, packed[...], moved)
    lane = lane[0:1]
    out[6:7, :] = jnp.where(lane < own + ghosts, 1.0, 0.0)
    out[7:8, :] = jnp.where(lane == 0, own + ghosts, 0).astype(F32)


def gather_stage(counts, start, offset, other_start, other_offset):
    vmem = pl.BlockSpec(memory_space=pltpu.VMEM)
    return pl.pallas_call(
        gather_kernel,
        out_shape=jax.ShapeDtypeStruct((8, ROWS), F32),
        in_specs=[
            pl.BlockSpec(memory_space=pltpu.SMEM),
            vmem,
            vmem,
            vmem,
            vmem,
        ],
        out_specs=vmem,
        scratch_shapes=[pltpu.VMEM((8, ROWS), F32)],
        name="gather_stage",
    )(counts, start, offset, other_start, other_offset)


def row_kernel(place, particles, table, near_table, phases, planes, phase, plane, sent_phase, sent_plane):
    y_cell = lax.broadcasted_iota(jnp.int32, (GRID, BLOCK), 0).astype(F32)
    support = lax.broadcasted_iota(jnp.int32, (SUPPORT, BLOCK), 0).astype(F32)
    x_cell = lax.broadcasted_iota(jnp.int32, (WINDOW, BLOCK), 0).astype(F32)
    local_z = lax.broadcasted_iota(jnp.int32, (16, BLOCK), 0)
    turn_of = local_z // 4
    c = 2 * (turn_of & 1) + turn_of // 2
    z_cell = (place[0] * 16 + 4 * (local_z % 4) + c).astype(F32)
    jobs = 2 * ((place[2] + 1) // 2)

    def copies(slot, job):
        return (
            pltpu.make_async_copy(phase.at[slot], phases.at[job], sent_phase.at[slot]),
            pltpu.make_async_copy(plane.at[slot], planes.at[job], sent_plane.at[slot]),
        )

    def one_job(job, carry):
        slot = job & (SLOTS - 1)

        @pl.when(job >= SLOTS)
        def _():
            for copy in copies(slot, job):
                copy.wait()

        entry, block = place[HEAD + job], place[HEAD + JOBS + job]
        owner = place[HEAD + 2 * JOBS + job]
        data = particles[entry, :, pl.ds(pl.multiple_of(block * BLOCK, BLOCK), BLOCK)]
        chosen = jnp.where(y_cell == data[1:2], 1.0, 0.0).astype(BF16)
        base = dot(table[...], jnp.concatenate([chosen, chosen], axis=0), NN)
        weight_y = weight(support, data[4:5])
        high = weight_y.astype(BF16).astype(F32)
        near = jnp.concatenate([high, weight_y - high, high, jnp.zeros_like(high)], axis=0)
        near = dot(near_table[...], near.astype(BF16), NN)
        phase[slot, 0:32] = base[0:32] * near[0:32] - base[32:64] * near[32:64]
        phase[slot, 32:64] = base[0:32] * near[32:64] + base[32:64] * near[0:32]
        weight_x = weight(x_cell + (owner * 32).astype(F32) - data[0:1], data[3:4])
        weight_z = weight(wrapped(z_cell - data[2:3]), data[5:6]) * data[6:7]
        for z in range(16):
            plane[slot, z * WINDOW : (z + 1) * WINDOW] = (weight_x * weight_z[z : z + 1]).astype(
                BF16
            )
        for copy in copies(slot, job):
            copy.start()
        return carry

    lax.fori_loop(0, jobs, one_job, 0)
    for slot in range(SLOTS):

        @pl.when(jobs > slot)
        def _():
            for copy in copies(slot, 0):
                copy.wait()


def row_stage(place, particles, table, near_table):
    return pl.pallas_call(
        row_kernel,
        out_shape=(
            jax.ShapeDtypeStruct((JOBS, 64, BLOCK), F32),
            jax.ShapeDtypeStruct((JOBS, 16 * WINDOW, BLOCK), BF16),
        ),
        grid_spec=pltpu.PrefetchScalarGridSpec(
            num_scalar_prefetch=1,
            grid=(1,),
            in_specs=[
                pl.BlockSpec((N_GY, 8, ROWS), lambda i, _: (0, 0, 0)),
                pl.BlockSpec((64, 512), lambda i, _: (0, 0)),
                pl.BlockSpec((64, 32), lambda i, _: (0, 0)),
            ],
            out_specs=(pl.BlockSpec(memory_space=pl.ANY), pl.BlockSpec(memory_space=pl.ANY)),
            scratch_shapes=[
                pltpu.VMEM((SLOTS, 64, BLOCK), F32),
                pltpu.VMEM((SLOTS, 16 * WINDOW, BLOCK), BF16),
                pltpu.SemaphoreType.DMA((SLOTS,)),
                pltpu.SemaphoreType.DMA((SLOTS,)),
            ],
        ),
        name="row_stage",
    )(place, particles, table, near_table)


def field_kernel(steps, place, main, extra, t_even, t_odd, phases, planes, *rest):
    previous = rest[0] if len(rest) == 11 else None
    out, field, work0, work1, work2, work3, window, phase, plane, arrived = rest[-10:]
    work = (work0, work1, work2, work3)
    first_c = ORDER.index(steps[0])
    depth = 4 * len(steps)
    step_c = pl.program_id(0)
    turn_of = first_c + step_c
    c = 2 * (turn_of & 1) + turn_of // 2
    pairs = (place[2] + 1) // 2

    def copies(pair, base):
        found = []
        for side in range(2):
            job, slot = 2 * pair + side, base + side
            rows = pl.ds(first_c * 4 * WINDOW, depth * WINDOW)
            found.append(
                pltpu.make_async_copy(phases.at[job], phase.at[slot], arrived.at[0, slot])
            )
            found.append(
                pltpu.make_async_copy(planes.at[job, rows], plane.at[slot], arrived.at[1, slot])
            )
        return found

    for ahead in range(AHEAD - 1):

        @pl.when((step_c == 0) & (pairs > ahead))
        def _():
            for copy in copies(ahead, 2 * ahead):
                copy.start()

    lane = lax.broadcasted_iota(jnp.int32, (HALF, 128), 1)
    group = lane // 32
    row = lax.broadcasted_iota(jnp.int32, (HALF, 128), 0)
    wave_y = WAVE * signed(lane % 32 + place[1] * 32)
    cross_y = jnp.where((group == 1) | (group == 3), 0.5 * wave_y, 0.0)
    half_same = jnp.where((group == 1) | (group == 2), 0.5, 0.0)
    plain_left = group == 2
    plain_extra = group == 3
    flat_main = main.reshape(GRID * 8, 128)
    flat_extra = extra.reshape(GRID * 8, 128)
    waves = [WAVE * signed(2 * row + parity) for parity in range(2)]
    for step in range(4):
        results = []
        for parity in range(2):
            target = work[2 * (step % 2) + parity]
            wave_x = waves[parity]
            cross_x = half_same * wave_x

            def load(flat, q):
                top = parity * 64 + q * 4 + step
                return jnp.concatenate(
                    [flat[pl.ds(source * 128 + top, 8, stride=8), :] for source in range(N_GX)]
                )

            parts = []
            for q in range(2):
                value = load(flat_main, q)
                moved = pltpu.roll(load(flat_extra, q), 32 * (3 - c), 1)
                left = pltpu.roll(value, 96, 1)
                right = pltpu.roll(value, 32, 1)
                cross = cross_y * right + cross_x * value
                plain = jnp.where(plain_left, left, jnp.where(plain_extra, moved, 0.0))
                parts.append((value, wave_x * left, cross, plain))
            (a_re, x_re, c_re, p_re), (a_im, x_im, c_im, p_im) = parts
            for top, left, value in (
                (0, 0, jnp.where(plain_extra, -x_im, a_re)),
                (HALF, 0, jnp.where(plain_extra, x_re, a_im)),
                (0, 128, p_re - c_im),
                (HALF, 128, p_im + c_re),
            ):
                high, low = split(value)
                lanes = slice(left, left + 128)
                target[top : top + HALF, lanes] = high
                target[GRID + top : GRID + top + HALF, lanes] = low
                target[2 * GRID + top : 2 * GRID + top + HALF, lanes] = high
            results.append(dot((t_even, t_odd)[parity][...], target[...], NN))
        from_even, from_odd = results
        near = (from_even + from_odd).astype(BF16)
        far = (from_even - from_odd).astype(BF16)
        z = step_c * 4 + step
        for q in range(2):
            lanes = slice(q * 256, q * 256 + 256)
            field[z, 0:HALF, lanes] = near[q * HALF : q * HALF + HALF]
            field[z, HALF:GRID, lanes] = far[q * HALF : q * HALF + HALF]
            field[z, GRID : GRID + 16, lanes] = near[q * HALF : q * HALF + 16]

    @pl.when(step_c == len(steps) - 1)
    def _():
        if previous is None:
            out[...] = jnp.zeros_like(out)
        else:
            out[...] = previous[...]

        for owner in range(N_GY):
            block = field[:, owner * 32 : owner * 32 + WINDOW, :]
            turned = block.reshape(depth * WINDOW, 512).T
            for q in range(2):
                top = q * 32 * FIELDS
                window[owner, top : top + 128] = turned[q * 256 : q * 256 + 128]
                window[owner, top + 128 : top + 224] = turned[q * 256 + 160 : q * 256 + 256]
        wave_rows = WAVE * signed(
            lax.broadcasted_iota(jnp.int32, (32, BLOCK), 0) + place[1] * 32
        )

        def one_pair(pair, carry):
            base = 2 * (pair & (AHEAD - 1))
            for copy in copies(pair, base):
                copy.wait()

            @pl.when(pair + AHEAD - 1 < pairs)
            def _():
                for copy in copies(pair + AHEAD - 1, 2 * ((pair + AHEAD - 1) & (AHEAD - 1))):
                    copy.start()

            for side in range(2):
                job = 2 * pair + side
                owner, block = place[HEAD + 2 * JOBS + job], place[HEAD + JOBS + job]
                lanes = pl.ds(pl.multiple_of(block * BLOCK, BLOCK), BLOCK)
                summed = dot(window[owner], plane[base + side], NN)
                summed = summed.reshape(2, FIELDS, 32, BLOCK)
                turn_re, turn_im = phase[base + side, 0:32], phase[base + side, 32:64]
                product = summed[0] * turn_re[None] + summed[1] * turn_im[None]
                along_y = wave_rows * (summed[0, 1] * turn_im - summed[1, 1] * turn_re)
                value = jnp.concatenate(
                    [jnp.sum(product, axis=1), jnp.sum(along_y, axis=0, keepdims=True)], axis=0
                )
                if previous is not None:
                    value = value + previous[owner, :, lanes]
                out[owner, :, lanes] = value
            return carry

        lax.fori_loop(0, pairs, one_pair, 0)


def field_stage(steps, first, place, main, extra, extra_at, t_even, t_odd, rows, previous):
    def whole(shape):
        return pl.BlockSpec(
            shape, lambda i, _: (0,) * len(shape), pipeline_mode=pl.Buffered(1)
        )

    def kernel(*refs):
        field_kernel(steps, *refs)

    piece = (N_GX, None, 2, 8, 8, 128)
    in_specs = [
        pl.BlockSpec(piece, lambda i, _: (0, first + i, 0, 0, 0, 0)),
        pl.BlockSpec(piece, lambda i, _: (0, extra_at, 0, 0, 0, 0)),
        whole((256, 768)),
        whole((256, 768)),
        pl.BlockSpec(memory_space=pl.ANY),
        pl.BlockSpec(memory_space=pl.ANY),
    ]
    operands = [place, main, extra, t_even, t_odd, *rows]
    if previous is not None:
        in_specs.append(whole((N_GY, 8, ROWS)))
        operands.append(previous)
    depth = 4 * len(steps)
    return pl.pallas_call(
        kernel,
        out_shape=jax.ShapeDtypeStruct((N_GY, 8, ROWS), F32),
        grid_spec=pltpu.PrefetchScalarGridSpec(
            num_scalar_prefetch=1,
            grid=(len(steps),),
            in_specs=in_specs,
            out_specs=whole((N_GY, 8, ROWS)),
            scratch_shapes=[
                pltpu.VMEM((depth, GRID + 16, 512), BF16),
                pltpu.VMEM((768, 256), BF16),
                pltpu.VMEM((768, 256), BF16),
                pltpu.VMEM((768, 256), BF16),
                pltpu.VMEM((768, 256), BF16),
                pltpu.VMEM((N_GY, 64 * FIELDS, depth * WINDOW), BF16),
                pltpu.VMEM((2 * AHEAD, 64, BLOCK), F32),
                pltpu.VMEM((2 * AHEAD, depth * WINDOW, BLOCK), BF16),
                pltpu.SemaphoreType.DMA((2, 2 * AHEAD)),
            ],
        ),
        name="field_stage",
    )(*operands)


def ghost_kernel(counts, values, slots, own, back):
    total = values[0]
    for source in range(1, N_GY):
        total = total + values[source]
    lane = lax.broadcasted_iota(jnp.int32, (8, OWN), 1)
    own[...] = jnp.where(lane < counts[0, 0], total[:, :OWN], 0.0)
    ghosts = pltpu.roll(total, ROWS - counts[0, 0], 1)[:, :GHOST]
    cell = lax.broadcasted_iota(jnp.int32, (OWN, GHOST), 0)
    chosen = (cell == slots[1:2]).astype(F32).astype(BF16)
    first, _ = split(ghosts)
    second, third = split(ghosts - first.astype(F32))
    parts = jnp.concatenate([first.astype(F32), second.astype(F32), third.astype(F32)], axis=0)
    placed = dot(parts.astype(BF16), chosen, NT)
    back[...] = placed[0:8] + (placed[8:16] + placed[16:24])


def ghost_stage(counts, values, slots):
    vmem = pl.BlockSpec(memory_space=pltpu.VMEM)
    return pl.pallas_call(
        ghost_kernel,
        out_shape=(
            jax.ShapeDtypeStruct((8, OWN), F32),
            jax.ShapeDtypeStruct((8, OWN), F32),
        ),
        in_specs=[pl.BlockSpec(memory_space=pltpu.SMEM), vmem, vmem],
        out_specs=(vmem, vmem),
        name="ghost_stage",
    )(counts, values, slots)


def final_kernel(own, arrived, velocity, strain):
    total = own[...] + arrived[...]
    velocity[...] = total[:3]
    strain[0:1] = total[3:4]
    strain[1:2] = total[7:8]
    strain[2:5] = total[4:7]


def final_stage(own, arrived):
    return pl.pallas_call(
        final_kernel,
        out_shape=(
            jax.ShapeDtypeStruct((3, OWN), F32),
            jax.ShapeDtypeStruct((5, OWN), F32),
        ),
        name="final_stage",
    )(own, arrived)


def job_list(live, owners, index_gx, index_gy):
    needed = (live + BLOCK - 1) // BLOCK
    valid = jnp.arange(BLOCKS, dtype=jnp.int32)[None, :] < needed[:, None]
    valid = valid.reshape(-1).astype(jnp.int32)
    item = jnp.arange(N_GY * BLOCKS, dtype=jnp.int32)
    before = jnp.sum(jnp.where(item[None, :] < item[:, None], valid[None, :], 0), axis=1)
    jobs = jnp.sum(valid)
    wanted = jnp.minimum(jnp.arange(JOBS, dtype=jnp.int32), jobs - 1)
    chosen = (before[None, :] == wanted[:, None]) & (valid[None, :] > 0)
    found = jnp.sum(jnp.where(chosen, item[None, :], 0), axis=1)
    entry = found // BLOCKS
    at_entry = entry[:, None] == jnp.arange(N_GY, dtype=jnp.int32)[None, :]
    owner = jnp.sum(jnp.where(at_entry, owners[None, :], 0), axis=1)
    return jnp.concatenate(
        [jnp.stack([index_gx, index_gy, jobs]), entry, found % BLOCKS, owner]
    )


def per_device(
    source_hat, particle_start, particle_offset, ghost_start, ghost_offset, ghost_slot, counts
):
    index_gx = lax.axis_index("gx").astype(jnp.int32)
    index_gy = lax.axis_index("gy").astype(jnp.int32)
    members = range(N_GY)
    mine = gather_stage(counts, particle_start, particle_offset, ghost_start, ghost_offset)
    partner = lax.ppermute(mine, "gy", [(i, i ^ 1) for i in members])

    table_z = jnp.asarray(left_triple(z_table()))
    twiddle = jnp.asarray(twiddles())
    groups = (CHUNKS[0] + (EXTRA,),) + CHUNKS[1:]
    sent = z_stage(groups, source_hat, table_z, twiddle)
    received = []
    for piece in sent:
        received.append(lax.all_to_all(piece, "gx", split_axis=0, concat_axis=0, tiled=True))
    pair = jnp.stack([mine, partner])
    pairs = [pair]
    for shift in (2, 6, 4):
        route = [(i, (i + shift) % N_GY) for i in members]
        pairs.append(lax.ppermute(pair, "gy", route))
    particles = jnp.concatenate(pairs, axis=0)
    shifts = jnp.array([0, 0, 2, 2, 6, 6, 4, 4], jnp.int32)
    owners = jnp.bitwise_xor(
        (index_gy - shifts) & (N_GY - 1), jnp.arange(N_GY, dtype=jnp.int32) & 1
    )
    place = job_list(particles[:, 7, 0].astype(jnp.int32), owners, index_gx, index_gy)
    tables_y = y_tables()
    table_y = lax.dynamic_index_in_dim(jnp.asarray(tables_y), index_gy, 0, keepdims=False)
    rows = row_stage(place, particles, table_y[:, :512], table_y[:, 512:])

    t_even = jnp.asarray(left_triple(x_table(0)))
    t_odd = jnp.asarray(left_triple(x_table(1)))
    partial = None
    for number, chunk in enumerate(CHUNKS):
        partial = field_stage(
            chunk, 0, place, received[number], received[0], len(CHUNKS[0]),
            t_even, t_odd, rows, partial,
        )
    partial = lax.all_to_all(partial, "gy", split_axis=0, concat_axis=0, tiled=True)
    own, back = ghost_stage(counts, partial, ghost_slot)
    devices = range(N_GX)
    route = [((i + 1) % N_GX, i) for i in devices]
    return final_stage(own, lax.ppermute(back, "gx", route))


def solution(mesh):
    in_specs = (
        P(None, None, "gx", "gy", None),
        P(None, ("gx", "gy")),
        P(None, ("gx", "gy")),
        P(None, None, ("gx", "gy")),
        P(None, None, ("gx", "gy")),
        P(None, ("gx", "gy")),
        P(("gx", "gy"), None),
    )
    out_specs = (P(None, ("gx", "gy")), P(None, ("gx", "gy")))
    return jax.shard_map(
        per_device, mesh=mesh, in_specs=in_specs, out_specs=out_specs, check_vma=False
    )
```

profile of v0, /device:TPU:1, one launch (start us, length us, event | category | flops | bytes accessed | tf_op | source)
XLA Modules:
  0.0 152.7 jit_solution(13093943978107061849)
XLA Ops:
  0.6 7.5 %z_stage.1 = f32[16,5,2,8,8,128]{5,4,3,2,1,0:T(8,128)} custom-call(f32[2,3,16,32,256]{4,3,2,1,0:T(8,128)} %refs_0_.1, bf16[256,768]{1,0:T(8,128)(2,1)} %constant.68.clone.refs_1_, f32[2,32,128]{2,1,0:T(8,128)} %constant.69.clone.refs_2_), custom_call_target="tpu_custom_call" | custom-call | tf_op jit(solution)/shard_map/z_stage/pallas_call | solution.py:200
  8.1 8.0 %all-to-all-start = ((f32[16,5,2,8,8,128]{5,4,3,2,1,0:T(8,128)}), f32[16,5,2,8,8,128]{5,4,3,2,1,0:T(8,128)}, u32[]{:S(2)}, u32[]{:S(2)}) async-start(f32[16,5,2,8,8,128]{5,4,3,2,1,0:T(8,128)} %z_stage.1), calls=%async_computation | async-start | bytes 10485760 | tf_op jit(solution)/shard_map/all_to_all | solution.py:608
  16.1 1.5 %gather_stage.1 = f32[8,2560]{1,0:T(8,128)} custom-call(s32[1,4]{1,0:T(1,128)} %counts.3, s32[3,2048]{1,0:T(4,128)} %start.1, f32[3,2048]{1,0:T(4,128)} %offset.1, s32[3,3,512]{2,1,0:T(4,128)} %other_start.1, f32[3,3,512]{2,1,0:T(4,128)} %other_offset.1), custom_call_target="tpu_custom_call" | custom-call | tf_op jit(solution)/shard_map/gather_stage/pallas_call | solution.py:247
  17.6 2.6 %collective-permute-start = (f32[8,2560]{1,0:T(8,128)}, f32[8,2560]{1,0:T(8,128)S(1)}, u32[]{:S(2)}, u32[]{:S(2)}) collective-permute-start(f32[8,2560]{1,0:T(8,128)} %gather_stage.1), channel_id=1, source_target_pairs={{0,1},{1,0},{2,3},{3,2},{4,5},{5,4},{6,7},{7,6},{8,9},{9,8},{10,11... | collective-permute-start | bytes 245768 | tf_op jit(solution)/shard_map/ppermute | solution.py:600
  20.3 0.9 constant_dynamic-update-slice_fusion.4
  21.2 0.9 dynamic-slice_bitcast_fusion
  22.1 0.6 slice.14.near_table
  22.7 0.6 slice.13.table
  23.3 56.0 %collective-permute-done = f32[8,2560]{1,0:T(8,128)S(1)} collective-permute-done((f32[8,2560]{1,0:T(8,128)}, f32[8,2560]{1,0:T(8,128)S(1)}, u32[]{:S(2)}, u32[]{:S(2)}) %collective-permute-start) | collective-permute-done | bytes 81952 | tf_op jit(solution)/shard_map/ppermute | solution.py:600
  79.3 0.9 pad_maximum_fusion
  80.2 2.8 %collective-permute-start.3 = (f32[2,8,2560]{2,1,0:T(8,128)S(1)}, f32[2,8,2560]{2,1,0:T(8,128)S(1)}, u32[]{:S(2)}, u32[]{:S(2)}) collective-permute-start(f32[2,8,2560]{2,1,0:T(8,128)S(1)} %pad_maximum_fusion), channel_id=1, source_target_pairs={{0,4},{1,5},{2,6},{3,7},{4,0},{5,1},{6,2},{7,3},{8,12},{9,13},{10,... | collective-permute-start | bytes 491528 | tf_op jit(solution)/shard_map/ppermute | solution.py:613
  83.0 0.9 collective-permute-start.2
  83.9 0.6 collective-permute-start.1
  84.5 6.5 %collective-permute-done.1 = f32[2,8,2560]{2,1,0:T(8,128)S(1)} collective-permute-done((f32[2,8,2560]{2,1,0:T(8,128)S(1)}, f32[2,8,2560]{2,1,0:T(8,128)S(1)}, u32[]{:S(2)}, u32[]{:S(2)}) %collective-permute-start.1) | collective-permute-done | bytes 163872 | tf_op jit(solution)/shard_map/ppermute | solution.py:613
  90.9 0.0 collective-permute-done.2
  91.0 0.0 collective-permute-done.3
  91.0 0.2 fusion.1
  91.3 0.1 fusion.2
  91.4 0.1 reshape.68
  91.4 0.8 fusion.3
  92.9 0.1 select_reduce_fusion.1
  93.0 0.1 select_reduce_fusion
  93.2 0.1 select_reduce_fusion.2
  93.3 1.4 concatenate.8.place.refs_0_
  94.6 9.9 %row_stage.1 = (f32[82,64,256]{2,1,0:T(8,128)}, bf16[82,768,256]{2,1,0:T(8,128)(2,1)}) custom-call(s32[249]{0:T(256)} %concatenate.8.place.refs_0_, f32[8,8,2560]{2,1,0:T(8,128)} %copy-done, bf16[64,512]{1,0:T(8,128)(2,1)} %slice.13.table, bf16[64,32]{1,0:T(8,128)(2,1)} %slice.14.near_table), custom_call_target="tpu_custom_call" | custom-call | tf_op jit(solution)/shard_map/row_stage/pallas_call | solution.py:318
  104.5 21.6 %field_stage.1 = f32[8,8,2560]{2,1,0:T(8,128)} custom-call(s32[249]{0:T(256)} %concatenate.8.place.refs_0_, f32[16,5,2,8,8,128]{5,4,3,2,1,0:T(8,128)} %all-to-all-done.refs_1_.refs_2_, f32[16,5,2,8,8,128]{5,4,3,2,1,0:T(8,128)} %all-to-all-done.refs_1_.refs_2_, bf16[256,768]{1,0:T(8,128)(2,1)} %constant.72.clone.refs_3_, ...), custom_call_target="tpu_custom_call" | custom-call | tf_op jit(solution)/shard_map/field_stage/pallas_call | solution.py:502
  126.2 14.5 %all_to_all.10.values = f32[8,8,2560]{2,1,0:T(8,128)} all-to-all(f32[8,8,2560]{2,1,0:T(8,128)} %field_stage.1), channel_id=1, replica_groups=mesh['gx'=16,'gy'=8] {'gy'}, dimensions={0} | all-to-all | bytes 1310720 | tf_op jit(solution)/shard_map/all_to_all | solution.py:632
  140.7 2.5 %ghost_stage.1 = (f32[8,2048]{1,0:T(8,128)}, f32[8,2048]{1,0:T(8,128)}) custom-call(s32[1,4]{1,0:T(1,128)} %counts.3, f32[8,8,2560]{2,1,0:T(8,128)} %all_to_all.10.values, s32[3,512]{1,0:T(4,128)} %slots.1), custom_call_target="tpu_custom_call" | custom-call | tf_op jit(solution)/shard_map/ghost_stage/pallas_call | solution.py:544
  143.2 4.1 %collective-permute-start.4 = (f32[8,2048]{1,0:T(8,128)}, f32[8,2048]{1,0:T(8,128)S(1)}, u32[]{:S(2)}, u32[]{:S(2)}) collective-permute-start(f32[8,2048]{1,0:T(8,128)} %get-tuple-element.9), channel_id=1, source_target_pairs={{8,0},{16,8},{24,16},{32,24},{40,32},{48,40},{56,48},{64,56},{72,6... | collective-permute-start | bytes 196616 | tf_op jit(solution)/shard_map/ppermute | solution.py:636
  147.3 3.3 %collective-permute-done.4.arrived = f32[8,2048]{1,0:T(8,128)S(1)} collective-permute-done((f32[8,2048]{1,0:T(8,128)}, f32[8,2048]{1,0:T(8,128)S(1)}, u32[]{:S(2)}, u32[]{:S(2)}) %collective-permute-start.4) | collective-permute-done | bytes 65568 | tf_op jit(solution)/shard_map/ppermute | solution.py:636
  150.6 0.6 copy-done.1
  151.2 1.5 final_stage.1
  (15 shorter events, 0.1 us)
Async XLA Ops:
  8.1 12.1 %copy-start.2 = (s32[8]{0:T(128)S(1)}, s32[8]{0:T(128)}, u32[]{:S(2)}) copy-start(s32[8]{0:T(128)} %constant.75) | copy-start | bytes 100
  8.1 96.4 %all-to-all-start = ((f32[16,5,2,8,8,128]{5,4,3,2,1,0:T(8,128)}), f32[16,5,2,8,8,128]{5,4,3,2,1,0:T(8,128)}, u32[]{:S(2)}, u32[]{:S(2)}) async-start(f32[16,5,2,8,8,128]{5,4,3,2,1,0:T(8,128)} %z_stage.1), calls=%async_computation | async-start | bytes 10485760 | tf_op jit(solution)/shard_map/all_to_all | solution.py:608
  17.6 61.6 %collective-permute-start = (f32[8,2560]{1,0:T(8,128)}, f32[8,2560]{1,0:T(8,128)S(1)}, u32[]{:S(2)}, u32[]{:S(2)}) collective-permute-start(f32[8,2560]{1,0:T(8,128)} %gather_stage.1), channel_id=1, source_target_pairs={{0,1},{1,0},{2,3},{3,2},{4,5},{5,4},{6,7},{7,6},{8,9},{9,8},{10,11... | collective-permute-start | bytes 245768 | tf_op jit(solution)/shard_map/ppermute | solution.py:600
  80.2 10.8 %collective-permute-start.3 = (f32[2,8,2560]{2,1,0:T(8,128)S(1)}, f32[2,8,2560]{2,1,0:T(8,128)S(1)}, u32[]{:S(2)}, u32[]{:S(2)}) collective-permute-start(f32[2,8,2560]{2,1,0:T(8,128)S(1)} %pad_maximum_fusion), channel_id=1, source_target_pairs={{0,4},{1,5},{2,6},{3,7},{4,0},{5,1},{6,2},{7,3},{8,12},{9,13},{10,... | collective-permute-start | bytes 491528 | tf_op jit(solution)/shard_map/ppermute | solution.py:613
  83.0 7.9 %collective-permute-start.2 = (f32[2,8,2560]{2,1,0:T(8,128)S(1)}, f32[2,8,2560]{2,1,0:T(8,128)S(1)}, u32[]{:S(2)}, u32[]{:S(2)}) collective-permute-start(f32[2,8,2560]{2,1,0:T(8,128)S(1)} %pad_maximum_fusion), channel_id=1, source_target_pairs={{0,6},{1,7},{2,0},{3,1},{4,2},{5,3},{6,4},{7,5},{8,14},{9,15},{10,... | collective-permute-start | bytes 491528 | tf_op jit(solution)/shard_map/ppermute | solution.py:613
  83.9 7.1 %collective-permute-start.1 = (f32[2,8,2560]{2,1,0:T(8,128)S(1)}, f32[2,8,2560]{2,1,0:T(8,128)S(1)}, u32[]{:S(2)}, u32[]{:S(2)}) collective-permute-start(f32[2,8,2560]{2,1,0:T(8,128)S(1)} %pad_maximum_fusion), channel_id=1, source_target_pairs={{0,2},{1,3},{2,4},{3,5},{4,6},{5,7},{6,0},{7,1},{8,10},{9,11},{10,... | collective-permute-start | bytes 491528 | tf_op jit(solution)/shard_map/ppermute | solution.py:613
  91.0 3.6 %copy-start = (f32[8,8,2560]{2,1,0:T(8,128)}, f32[8,8,2560]{2,1,0:T(8,128)S(1)}, u32[]{:S(2)}) copy-start(f32[8,8,2560]{2,1,0:T(8,128)S(1)} %constant_dynamic-update-slice_fusion.particles) | copy-start | bytes 1966084
  143.2 7.4 %collective-permute-start.4 = (f32[8,2048]{1,0:T(8,128)}, f32[8,2048]{1,0:T(8,128)S(1)}, u32[]{:S(2)}, u32[]{:S(2)}) collective-permute-start(f32[8,2048]{1,0:T(8,128)} %get-tuple-element.9), channel_id=1, source_target_pairs={{8,0},{16,8},{24,16},{32,24},{40,32},{48,40},{56,48},{64,56},{72,6... | collective-permute-start | bytes 196616 | tf_op jit(solution)/shard_map/ppermute | solution.py:636
  150.6 0.6 copy-start.1
where the time goes:
time: 153 us
  waiting for transfers between devices  65.7 us (43%)
  Pallas kernels  44.6 us (29%)
  starting transfers between devices  19 us (12%)
  blocking collectives  14.5 us (9%)
  local copies, waits for them, and re-layouts  5.18 us (3%)
  other arithmetic  2.34 us (2%)
    ppermute x1, waiting for transfers between devices, per_device(): partner = lax.ppermute(mine, 'gy', [(i, i ^ 1) for i in members])  56 us
    pallas_call x1, Pallas kernels, field_stage(): pl.pallas_call(kernel, out_shape=jax.ShapeDtypeStruct((N_GY, 8, ROWS), F3...  21.6 us
    all_to_all x1, blocking collectives, per_device(): lax.all_to_all(partial, 'gy', split_axis=0, concat_axis=0, tiled=True)  14.5 us
    pallas_call x1, Pallas kernels, row_stage(): pl.pallas_call(row_kernel, out_shape=(jax.ShapeDtypeStruct((JOBS, 64, BLO...  9.88 us
    all_to_all x1, starting transfers between devices, per_device(): lax.all_to_all(piece, 'gx', split_axis=0, concat_axis=0, tiled=True)  7.96 us
    pallas_call x1, Pallas kernels, z_stage(): pl.pallas_call(kernel, out_shape=tuple((jax.ShapeDtypeStruct((N_GX, len(g...  7.51 us
    ppermute x3, waiting for transfers between devices, per_device(): pairs.append(lax.ppermute(pair, 'gy', route))  6.46 us
    ppermute x3, starting transfers between devices, per_device(): pairs.append(lax.ppermute(pair, 'gy', route))  4.29 us
  transfers between devices with their start and end apart: 6, of which 3 were waited for; matrix products, arithmetic and copies ran while one was open for 5% of the time, Pallas kernels for 7%

commit v1 on v0

--- a/solution.py
+++ b/solution.py
@@ -531,7 +531,7 @@
     own[...] = jnp.where(lane < counts[0, 0], total[:, :OWN], 0.0)
     ghosts = pltpu.roll(total, ROWS - counts[0, 0], 1)[:, :GHOST]
     cell = lax.broadcasted_iota(jnp.int32, (OWN, GHOST), 0)
-    chosen = (cell == slots[1:2]).astype(F32).astype(BF16)
+    chosen = jnp.where(cell == slots[1:2], 1.0, 0.0).astype(BF16)
     first, _ = split(ghosts)
     second, third = split(ghosts - first.astype(F32))
     parts = jnp.concatenate([first.astype(F32), second.astype(F32), third.astype(F32)], axis=0)
@@ -562,12 +562,15 @@
 
 
 def final_stage(own, arrived):
+    vmem = pl.BlockSpec(memory_space=pltpu.VMEM)
     return pl.pallas_call(
         final_kernel,
         out_shape=(
             jax.ShapeDtypeStruct((3, OWN), F32),
             jax.ShapeDtypeStruct((5, OWN), F32),
         ),
+        in_specs=[vmem, vmem],
+        out_specs=(vmem, vmem),
         name="final_stage",
     )(own, arrived)
 

time: 153 us -> 153 us (level)
  no operation moved by 1% of the time
where the time goes in v1:
time: 153 us
  waiting for transfers between devices  65.7 us (43%)
  Pallas kernels  44.6 us (29%)
  starting transfers between devices  19 us (12%)
  blocking collectives  14.5 us (9%)
  local copies, waits for them, and re-layouts  5.18 us (3%)
  other arithmetic  2.34 us (2%)
    ppermute x1, waiting for transfers between devices, per_device(): partner = lax.ppermute(mine, 'gy', [(i, i ^ 1) for i in members])  56 us
    pallas_call x1, Pallas kernels, field_stage(): pl.pallas_call(kernel, out_shape=jax.ShapeDtypeStruct((N_GY, 8, ROWS), F3...  21.6 us
    all_to_all x1, blocking collectives, per_device(): lax.all_to_all(partial, 'gy', split_axis=0, concat_axis=0, tiled=True)  14.5 us
    pallas_call x1, Pallas kernels, row_stage(): pl.pallas_call(row_kernel, out_shape=(jax.ShapeDtypeStruct((JOBS, 64, BLO...  9.88 us
    all_to_all x1, starting transfers between devices, per_device(): lax.all_to_all(piece, 'gx', split_axis=0, concat_axis=0, tiled=True)  7.96 us
    pallas_call x1, Pallas kernels, z_stage(): pl.pallas_call(kernel, out_shape=tuple((jax.ShapeDtypeStruct((N_GX, len(g...  7.51 us
    ppermute x3, waiting for transfers between devices, per_device(): pairs.append(lax.ppermute(pair, 'gy', route))  6.46 us
    ppermute x3, starting transfers between devices, per_device(): pairs.append(lax.ppermute(pair, 'gy', route))  4.29 us
  transfers between devices with their start and end apart: 6, of which 3 were waited for; matrix products, arithmetic and copies ran while one was open for 5% of the time, Pallas kernels for 7%

profile of v1, /device:TPU:1, one launch (start us, length us, event | category | flops | bytes accessed | tf_op | source)
XLA Modules:
  0.0 152.7 jit_solution(13093943978107061849)
XLA Ops:
  0.6 7.5 %z_stage.1 = f32[16,5,2,8,8,128]{5,4,3,2,1,0:T(8,128)} custom-call(f32[2,3,16,32,256]{4,3,2,1,0:T(8,128)} %refs_0_.1, bf16[256,768]{1,0:T(8,128)(2,1)} %constant.68.clone.refs_1_, f32[2,32,128]{2,1,0:T(8,128)} %constant.69.clone.refs_2_), custom_call_target="tpu_custom_call" | custom-call | tf_op jit(solution)/shard_map/z_stage/pallas_call | solution.py:200
  8.1 8.0 %all-to-all-start = ((f32[16,5,2,8,8,128]{5,4,3,2,1,0:T(8,128)}), f32[16,5,2,8,8,128]{5,4,3,2,1,0:T(8,128)}, u32[]{:S(2)}, u32[]{:S(2)}) async-start(f32[16,5,2,8,8,128]{5,4,3,2,1,0:T(8,128)} %z_stage.1), calls=%async_computation | async-start | bytes 10485760 | tf_op jit(solution)/shard_map/all_to_all | solution.py:611
  16.1 1.5 %gather_stage.1 = f32[8,2560]{1,0:T(8,128)} custom-call(s32[1,4]{1,0:T(1,128)} %counts.3, s32[3,2048]{1,0:T(4,128)} %start.1, f32[3,2048]{1,0:T(4,128)} %offset.1, s32[3,3,512]{2,1,0:T(4,128)} %other_start.1, f32[3,3,512]{2,1,0:T(4,128)} %other_offset.1), custom_call_target="tpu_custom_call" | custom-call | tf_op jit(solution)/shard_map/gather_stage/pallas_call | solution.py:247
  17.6 2.6 %collective-permute-start = (f32[8,2560]{1,0:T(8,128)}, f32[8,2560]{1,0:T(8,128)S(1)}, u32[]{:S(2)}, u32[]{:S(2)}) collective-permute-start(f32[8,2560]{1,0:T(8,128)} %gather_stage.1), channel_id=1, source_target_pairs={{0,1},{1,0},{2,3},{3,2},{4,5},{5,4},{6,7},{7,6},{8,9},{9,8},{10,11... | collective-permute-start | bytes 245768 | tf_op jit(solution)/shard_map/ppermute | solution.py:603
  20.3 0.9 constant_dynamic-update-slice_fusion.4
  21.2 0.9 dynamic-slice_bitcast_fusion
  22.1 0.6 slice.14.near_table
  22.7 0.6 slice.13.table
  23.3 56.0 %collective-permute-done = f32[8,2560]{1,0:T(8,128)S(1)} collective-permute-done((f32[8,2560]{1,0:T(8,128)}, f32[8,2560]{1,0:T(8,128)S(1)}, u32[]{:S(2)}, u32[]{:S(2)}) %collective-permute-start) | collective-permute-done | bytes 81952 | tf_op jit(solution)/shard_map/ppermute | solution.py:603
  79.3 0.9 pad_maximum_fusion
  80.2 2.8 %collective-permute-start.3 = (f32[2,8,2560]{2,1,0:T(8,128)S(1)}, f32[2,8,2560]{2,1,0:T(8,128)S(1)}, u32[]{:S(2)}, u32[]{:S(2)}) collective-permute-start(f32[2,8,2560]{2,1,0:T(8,128)S(1)} %pad_maximum_fusion), channel_id=1, source_target_pairs={{0,4},{1,5},{2,6},{3,7},{4,0},{5,1},{6,2},{7,3},{8,12},{9,13},{10,... | collective-permute-start | bytes 491528 | tf_op jit(solution)/shard_map/ppermute | solution.py:616
  83.0 0.9 collective-permute-start.2
  83.9 0.6 collective-permute-start.1
  84.5 6.5 %collective-permute-done.1 = f32[2,8,2560]{2,1,0:T(8,128)S(1)} collective-permute-done((f32[2,8,2560]{2,1,0:T(8,128)S(1)}, f32[2,8,2560]{2,1,0:T(8,128)S(1)}, u32[]{:S(2)}, u32[]{:S(2)}) %collective-permute-start.1) | collective-permute-done | bytes 163872 | tf_op jit(solution)/shard_map/ppermute | solution.py:616
  90.9 0.0 collective-permute-done.2
  91.0 0.0 collective-permute-done.3
  91.0 0.2 fusion.1
  91.3 0.1 fusion.2
  91.4 0.1 reshape.68
  91.4 0.8 fusion.3
  92.9 0.1 select_reduce_fusion.1
  93.0 0.1 select_reduce_fusion
  93.2 0.1 select_reduce_fusion.2
  93.3 1.4 concatenate.8.place.refs_0_
  94.6 9.9 %row_stage.1 = (f32[82,64,256]{2,1,0:T(8,128)}, bf16[82,768,256]{2,1,0:T(8,128)(2,1)}) custom-call(s32[249]{0:T(256)} %concatenate.8.place.refs_0_, f32[8,8,2560]{2,1,0:T(8,128)} %copy-done, bf16[64,512]{1,0:T(8,128)(2,1)} %slice.13.table, bf16[64,32]{1,0:T(8,128)(2,1)} %slice.14.near_table), custom_call_target="tpu_custom_call" | custom-call | tf_op jit(solution)/shard_map/row_stage/pallas_call | solution.py:318
  104.5 21.6 %field_stage.1 = f32[8,8,2560]{2,1,0:T(8,128)} custom-call(s32[249]{0:T(256)} %concatenate.8.place.refs_0_, f32[16,5,2,8,8,128]{5,4,3,2,1,0:T(8,128)} %all-to-all-done.refs_1_.refs_2_, f32[16,5,2,8,8,128]{5,4,3,2,1,0:T(8,128)} %all-to-all-done.refs_1_.refs_2_, bf16[256,768]{1,0:T(8,128)(2,1)} %constant.72.clone.refs_3_, ...), custom_call_target="tpu_custom_call" | custom-call | tf_op jit(solution)/shard_map/field_stage/pallas_call | solution.py:502
  126.2 14.5 %all_to_all.10.values = f32[8,8,2560]{2,1,0:T(8,128)} all-to-all(f32[8,8,2560]{2,1,0:T(8,128)} %field_stage.1), channel_id=1, replica_groups=mesh['gx'=16,'gy'=8] {'gy'}, dimensions={0} | all-to-all | bytes 1310720 | tf_op jit(solution)/shard_map/all_to_all | solution.py:635
  140.7 2.5 %ghost_stage.1 = (f32[8,2048]{1,0:T(8,128)}, f32[8,2048]{1,0:T(8,128)}) custom-call(s32[1,4]{1,0:T(1,128)} %counts.3, f32[8,8,2560]{2,1,0:T(8,128)} %all_to_all.10.values, s32[3,512]{1,0:T(4,128)} %slots.1), custom_call_target="tpu_custom_call" | custom-call | tf_op jit(solution)/shard_map/ghost_stage/pallas_call | solution.py:544
  143.2 4.1 %collective-permute-start.4 = (f32[8,2048]{1,0:T(8,128)}, f32[8,2048]{1,0:T(8,128)S(1)}, u32[]{:S(2)}, u32[]{:S(2)}) collective-permute-start(f32[8,2048]{1,0:T(8,128)} %get-tuple-element.9), channel_id=1, source_target_pairs={{8,0},{16,8},{24,16},{32,24},{40,32},{48,40},{56,48},{64,56},{72,6... | collective-permute-start | bytes 196616 | tf_op jit(solution)/shard_map/ppermute | solution.py:639
  147.3 3.3 %collective-permute-done.4.arrived = f32[8,2048]{1,0:T(8,128)S(1)} collective-permute-done((f32[8,2048]{1,0:T(8,128)}, f32[8,2048]{1,0:T(8,128)S(1)}, u32[]{:S(2)}, u32[]{:S(2)}) %collective-permute-start.4) | collective-permute-done | bytes 65568 | tf_op jit(solution)/shard_map/ppermute | solution.py:639
  150.6 0.6 copy-done.1
  151.2 1.5 final_stage.1
  (15 shorter events, 0.1 us)
Async XLA Ops:
  8.1 12.1 %copy-start.2 = (s32[8]{0:T(128)S(1)}, s32[8]{0:T(128)}, u32[]{:S(2)}) copy-start(s32[8]{0:T(128)} %constant.75) | copy-start | bytes 100
  8.1 96.4 %all-to-all-start = ((f32[16,5,2,8,8,128]{5,4,3,2,1,0:T(8,128)}), f32[16,5,2,8,8,128]{5,4,3,2,1,0:T(8,128)}, u32[]{:S(2)}, u32[]{:S(2)}) async-start(f32[16,5,2,8,8,128]{5,4,3,2,1,0:T(8,128)} %z_stage.1), calls=%async_computation | async-start | bytes 10485760 | tf_op jit(solution)/shard_map/all_to_all | solution.py:611
  17.6 61.6 %collective-permute-start = (f32[8,2560]{1,0:T(8,128)}, f32[8,2560]{1,0:T(8,128)S(1)}, u32[]{:S(2)}, u32[]{:S(2)}) collective-permute-start(f32[8,2560]{1,0:T(8,128)} %gather_stage.1), channel_id=1, source_target_pairs={{0,1},{1,0},{2,3},{3,2},{4,5},{5,4},{6,7},{7,6},{8,9},{9,8},{10,11... | collective-permute-start | bytes 245768 | tf_op jit(solution)/shard_map/ppermute | solution.py:603
  80.2 10.8 %collective-permute-start.3 = (f32[2,8,2560]{2,1,0:T(8,128)S(1)}, f32[2,8,2560]{2,1,0:T(8,128)S(1)}, u32[]{:S(2)}, u32[]{:S(2)}) collective-permute-start(f32[2,8,2560]{2,1,0:T(8,128)S(1)} %pad_maximum_fusion), channel_id=1, source_target_pairs={{0,4},{1,5},{2,6},{3,7},{4,0},{5,1},{6,2},{7,3},{8,12},{9,13},{10,... | collective-permute-start | bytes 491528 | tf_op jit(solution)/shard_map/ppermute | solution.py:616
  83.0 7.9 %collective-permute-start.2 = (f32[2,8,2560]{2,1,0:T(8,128)S(1)}, f32[2,8,2560]{2,1,0:T(8,128)S(1)}, u32[]{:S(2)}, u32[]{:S(2)}) collective-permute-start(f32[2,8,2560]{2,1,0:T(8,128)S(1)} %pad_maximum_fusion), channel_id=1, source_target_pairs={{0,6},{1,7},{2,0},{3,1},{4,2},{5,3},{6,4},{7,5},{8,14},{9,15},{10,... | collective-permute-start | bytes 491528 | tf_op jit(solution)/shard_map/ppermute | solution.py:616
  83.9 7.1 %collective-permute-start.1 = (f32[2,8,2560]{2,1,0:T(8,128)S(1)}, f32[2,8,2560]{2,1,0:T(8,128)S(1)}, u32[]{:S(2)}, u32[]{:S(2)}) collective-permute-start(f32[2,8,2560]{2,1,0:T(8,128)S(1)} %pad_maximum_fusion), channel_id=1, source_target_pairs={{0,2},{1,3},{2,4},{3,5},{4,6},{5,7},{6,0},{7,1},{8,10},{9,11},{10,... | collective-permute-start | bytes 491528 | tf_op jit(solution)/shard_map/ppermute | solution.py:616
  91.0 3.6 %copy-start = (f32[8,8,2560]{2,1,0:T(8,128)}, f32[8,8,2560]{2,1,0:T(8,128)S(1)}, u32[]{:S(2)}) copy-start(f32[8,8,2560]{2,1,0:T(8,128)S(1)} %constant_dynamic-update-slice_fusion.particles) | copy-start | bytes 1966084
  143.2 7.4 %collective-permute-start.4 = (f32[8,2048]{1,0:T(8,128)}, f32[8,2048]{1,0:T(8,128)S(1)}, u32[]{:S(2)}, u32[]{:S(2)}) collective-permute-start(f32[8,2048]{1,0:T(8,128)} %get-tuple-element.9), channel_id=1, source_target_pairs={{8,0},{16,8},{24,16},{32,24},{40,32},{48,40},{56,48},{64,56},{72,6... | collective-permute-start | bytes 196616 | tf_op jit(solution)/shard_map/ppermute | solution.py:639
  150.6 0.6 copy-start.1
